TPU v7x, 32 devices: a whole 2x2x4 slice. The times are simulated.
32 devices in a mesh: rep: 4 (over x, core), shard: 8 (over z, y).
Axes of the slice: x: 2, y: 2, z: 4, core: 2. Of those that a mesh axis runs over, the one named last changes fastest.
Arguments:
- inputs: bfloat16 [32, 1024, 512], P(('rep', 'shard')), may hold values from -6 to 6
- segments: int32 [32, 1024], P(('rep', 'shard')), may hold values from 0 to 7, never falling along the last dimension, each value on 1 to 512 neighbouring positions
- valid_mask: int32 [32, 1024], P(('rep', 'shard')), may hold values from 0 to 1, as said below
- teacher: bfloat16 [32, 1024, 512], P(('rep', 'shard')), may hold values from -6 to 6
- query_weight: bfloat16 [512, 512], P('shard'), may hold values from -0.5 to 0.5
- key_weight: bfloat16 [512, 512], P('shard'), may hold values from -0.25 to 0.25
- value_weight: bfloat16 [512, 512], P('shard'), may hold values from -0.25 to 0.25
- control_weight: bfloat16 [512, 512], P('shard'), may hold values from -0.75 to 0.75
- output_weight: bfloat16 [512, 512], P('shard'), may hold values from -0.75 to 0.75
- gain_first: bfloat16 [512], P('shard'), may hold values from 0.5 to 1.5
- shift_first: bfloat16 [512], P('shard'), may hold values from -4 to 4
- expand_weight: bfloat16 [512, 2048], P('shard'), may hold values from -0.25 to 0.25
- expand_bias: bfloat16 [2048], P('shard'), may hold values from -4 to 4
- contract_weight: bfloat16 [2048, 512], P('shard'), may hold values from -0.1875 to 0.1875
- contract_bias: bfloat16 [512], P('shard'), may hold values from -4 to 4
- gain_second: bfloat16 [512], P('shard'), may hold values from 0.5 to 1.5
- shift_second: bfloat16 [512], P('shard'), may hold values from -4 to 4
Outputs:
- layer_out: bfloat16 [32, 1024, 512], P(('rep', 'shard'))
- grad_inputs: float32 [32, 1024, 512], P(('rep', 'shard'))
- loss_value: float32 [], replicated
- grad_query_weight: float32 [512, 512], P('shard')
- grad_key_weight: float32 [512, 512], P('shard')
- grad_value_weight: float32 [512, 512], P('shard')
- grad_control_weight: float32 [512, 512], P('shard')
- grad_output_weight: float32 [512, 512], P('shard')
- grad_gain_first: float32 [512], P('shard')
- grad_shift_first: float32 [512], P('shard')
- grad_expand_weight: float32 [512, 2048], P('shard')
- grad_expand_bias: float32 [2048], P('shard')
- grad_contract_weight: float32 [2048, 512], P('shard')
- grad_contract_bias: float32 [512], P('shard')
- grad_gain_second: float32 [512], P('shard')
- grad_shift_second: float32 [512], P('shard')
Inputs may be any that keep to these rules, and one draw needn't show every extreme that they name: `valid_mask`: 1 marks a token that counts toward the loss; the first token of every sequence always counts. `segments`: within each sequence ids start at 0 and never fall; each document has 1 to 512 tokens, and one has exactly 512.
All inputs are finite; a program needn't handle non-finite values.
Results may differ from a plain program's by a relative error of at most 0.017.
Values may be sent and summed in bfloat16 or wider, within the bound.
No kernel may reach another device: no remote copies, remote signals or barrier semaphores. Data moves between devices by JAX's collectives and lax.ppermute only.
A program may use at most 128 MiB of HBM per device.

v0:
```python
from functools import partial
import jax
import jax.numpy as jnp
from jax import lax
from jax.sharding import PartitionSpec as P

HEADS = 8
EPSILON = 1e-05
HIGHEST = lax.Precision.HIGHEST
THREEPASS = lax.Precision.HIGH


def layer_norm(activations, gain, shift):
    row_mean = jnp.mean(activations, axis=-1, keepdims=True)
    centred = activations - row_mean
    variance = jnp.mean(centred * centred, axis=-1, keepdims=True)
    return centred * lax.rsqrt(variance + EPSILON) * gain + shift


def doc_mask(segment_row):
    places = jnp.arange(segment_row.shape[0], dtype=jnp.int32)
    earlier = places[None, :] <= places[:, None]
    same_document = segment_row[:, None] == segment_row[None, :]
    return jnp.where(earlier & same_document, 1.0, 0.0).astype(jnp.bfloat16)


def product(left, right):
    return jnp.dot(left, right, preferred_element_type=jnp.float32)


def head_scores(queries, key_rows):
    return product(queries, key_rows.T) * queries.shape[-1] ** (-0.5)


def slot_rest(causal, scores, value_rows, control):
    weights = jnp.exp(control)
    totals = jnp.dot(causal, weights, precision=THREEPASS, preferred_element_type=jnp.float32)
    slot_scores = jnp.dot(scores * causal, weights, precision=HIGHEST) / totals
    slot_shares = jax.nn.softmax(slot_scores, axis=-1)
    mixing = jnp.dot(slot_shares / totals, weights.T, precision=HIGHEST) * causal
    return jnp.dot(mixing, value_rows, precision=THREEPASS, preferred_element_type=jnp.float32)


def head_forward(causal, head_bundle):
    queries, key_rows, value_rows, control = head_bundle
    return slot_rest(causal, head_scores(queries, key_rows), value_rows, control)


def head_backward(causal, head_bundle):
    queries, key_rows, value_rows, control, grad_mixed = head_bundle
    scores = head_scores(queries, key_rows)
    outcome, pullback = jax.vjp(partial(slot_rest, causal), scores, value_rows, control)
    grad_scores, grad_values, grad_control = pullback(grad_mixed)
    scale = queries.shape[-1] ** (-0.5)
    grad_queries = (
        jnp.dot(grad_scores, key_rows, precision=THREEPASS, preferred_element_type=jnp.float32)
        * scale
    )
    grad_keys = (
        jnp.dot(grad_scores.T, queries, precision=THREEPASS, preferred_element_type=jnp.float32)
        * scale
    )
    return (grad_queries, grad_keys, grad_values.astype(jnp.float32), grad_control)


def mix_forward(bundle):
    queries, key_rows, value_rows, control, segment_row = bundle
    causal = doc_mask(segment_row)
    return lax.map(partial(head_forward, causal), (queries, key_rows, value_rows, control))


def mix_backward(bundle):
    queries, key_rows, value_rows, control, grad_mixed, segment_row = bundle
    causal = doc_mask(segment_row)
    return lax.map(
        partial(head_backward, causal), (queries, key_rows, value_rows, control, grad_mixed)
    )


def split_heads(matrix, sequence_count):
    return matrix.reshape(sequence_count, -1, HEADS, matrix.shape[1] // HEADS).transpose(0, 2, 1, 3)


def merge_heads(stacked):
    sequence_count, head_count, length, head_width = stacked.shape
    return stacked.transpose(0, 2, 1, 3).reshape(sequence_count * length, head_count * head_width)


def local(
    inputs,
    segments,
    valid_mask,
    teacher,
    query_weight,
    key_weight,
    value_weight,
    control_weight,
    output_weight,
    gain_first,
    shift_first,
    expand_weight,
    expand_bias,
    contract_weight,
    contract_bias,
    gain_second,
    shift_second,
):
    sequence_count, length, width = inputs.shape
    total_rows = sequence_count * length
    valid_rows = valid_mask.reshape(total_rows, 1).astype(jnp.float32)
    local_count = jnp.sum(valid_rows)
    count_all = lax.psum(local_count, ("rep", "shard"))
    mixer_set = (
        lax.all_gather(query_weight, "shard", axis=0, tiled=True),
        lax.all_gather(key_weight, "shard", axis=0, tiled=True),
        lax.all_gather(value_weight, "shard", axis=0, tiled=True),
        lax.all_gather(control_weight, "shard", axis=0, tiled=True),
        lax.all_gather(output_weight, "shard", axis=0, tiled=True),
        lax.all_gather(gain_first, "shard", axis=0, tiled=True),
        lax.all_gather(shift_first, "shard", axis=0, tiled=True),
    )
    query_full, key_full, value_full, control_full, out_full, gain_one, shift_one = mixer_set
    layer_in = inputs.reshape(total_rows, width).astype(jnp.float32)
    normed_one, first_back = jax.vjp(
        layer_norm, layer_in, gain_one.astype(jnp.float32), shift_one.astype(jnp.float32)
    )
    normed_one = normed_one.astype(jnp.bfloat16)
    queries = product(normed_one, query_full).astype(jnp.bfloat16)
    key_rows = product(normed_one, key_full).astype(jnp.bfloat16)
    value_rows = product(normed_one, value_full).astype(jnp.bfloat16)
    control = product(normed_one, control_full)
    head_queries = split_heads(queries, sequence_count)
    head_keys = split_heads(key_rows, sequence_count)
    head_values = split_heads(value_rows, sequence_count)
    head_control = split_heads(control, sequence_count)
    mixed = lax.map(mix_forward, (head_queries, head_keys, head_values, head_control, segments))
    mixed_low = merge_heads(mixed).astype(jnp.bfloat16)
    hidden_one = layer_in + product(mixed_low, out_full)
    branch_set = (
        lax.all_gather(expand_weight, "shard", axis=0, tiled=True),
        lax.all_gather(expand_bias, "shard", axis=0, tiled=True),
        lax.all_gather(contract_weight, "shard", axis=0, tiled=True),
        lax.all_gather(contract_bias, "shard", axis=0, tiled=True),
        lax.all_gather(gain_second, "shard", axis=0, tiled=True),
        lax.all_gather(shift_second, "shard", axis=0, tiled=True),
    )
    expand_full, expand_shift, contract_full, contract_shift, gain_two, shift_two = branch_set
    normed_two, second_back = jax.vjp(
        layer_norm, hidden_one, gain_two.astype(jnp.float32), shift_two.astype(jnp.float32)
    )
    normed_two = normed_two.astype(jnp.bfloat16)
    before_relu = product(normed_two, expand_full) + expand_shift.astype(jnp.float32)
    after_relu = jnp.maximum(before_relu, 0.0).astype(jnp.bfloat16)
    result = hidden_one + (product(after_relu, contract_full) + contract_shift.astype(jnp.float32))
    layer_out = result.astype(jnp.bfloat16).reshape(sequence_count, length, width)
    error = result - teacher.reshape(total_rows, width).astype(jnp.float32)
    local_loss = jnp.sum(valid_rows * error * error)
    loss_all = lax.psum(local_loss, ("rep", "shard"))
    loss_value = loss_all / (2.0 * count_all)
    total_tokens = total_rows * lax.axis_size("rep") * lax.axis_size("shard")
    grad_result = total_tokens / count_all * valid_rows * error
    branch_set = (
        lax.all_gather(expand_weight, "shard", axis=0, tiled=True),
        lax.all_gather(expand_bias, "shard", axis=0, tiled=True),
        lax.all_gather(contract_weight, "shard", axis=0, tiled=True),
        lax.all_gather(contract_bias, "shard", axis=0, tiled=True),
        lax.all_gather(gain_second, "shard", axis=0, tiled=True),
        lax.all_gather(shift_second, "shard", axis=0, tiled=True),
    )
    expand_full, expand_shift, contract_full, contract_shift, gain_two, shift_two = branch_set
    grad_second_low = grad_result.astype(jnp.bfloat16)
    grad_contract = product(after_relu.T, grad_second_low)
    grad_contract_shift = jnp.sum(grad_second_low.astype(jnp.float32), axis=0)
    grad_after = product(grad_second_low, contract_full.T)
    grad_before = jnp.where(before_relu > 0, grad_after, 0.0).astype(jnp.bfloat16)
    grad_expand = product(normed_two.T, grad_before)
    grad_expand_shift = jnp.sum(grad_before.astype(jnp.float32), axis=0)
    grad_normed_two = product(grad_before, expand_full.T)
    grad_hidden_part, grad_gain_two, grad_shift_two = second_back(grad_normed_two)
    grad_hidden = grad_result + grad_hidden_part
    mixer_set = (
        lax.all_gather(query_weight, "shard", axis=0, tiled=True),
        lax.all_gather(key_weight, "shard", axis=0, tiled=True),
        lax.all_gather(value_weight, "shard", axis=0, tiled=True),
        lax.all_gather(control_weight, "shard", axis=0, tiled=True),
        lax.all_gather(output_weight, "shard", axis=0, tiled=True),
        lax.all_gather(gain_first, "shard", axis=0, tiled=True),
        lax.all_gather(shift_first, "shard", axis=0, tiled=True),
    )
    query_full, key_full, value_full, control_full, out_full, gain_one, shift_one = mixer_set
    grad_mixer_low = grad_hidden.astype(jnp.bfloat16)
    grad_output = product(mixed_low.T, grad_mixer_low)
    grad_mixed = product(grad_mixer_low, out_full.T)
    head_grads = lax.map(
        mix_backward,
        (
            head_queries,
            head_keys,
            head_values,
            head_control,
            split_heads(grad_mixed, sequence_count),
            segments,
        ),
    )
    grad_queries = merge_heads(head_grads[0]).astype(jnp.bfloat16)
    grad_key_rows = merge_heads(head_grads[1]).astype(jnp.bfloat16)
    grad_value_rows = merge_heads(head_grads[2]).astype(jnp.bfloat16)
    grad_control = merge_heads(head_grads[3]).astype(jnp.bfloat16)
    grad_query = product(normed_one.T, grad_queries)
    grad_key = product(normed_one.T, grad_key_rows)
    grad_value = product(normed_one.T, grad_value_rows)
    grad_control_full = product(normed_one.T, grad_control)
    grad_normed_one = (
        product(grad_queries, query_full.T)
        + product(grad_key_rows, key_full.T)
        + product(grad_value_rows, value_full.T)
        + product(grad_control, control_full.T)
    )
    grad_layer_in, grad_gain_one, grad_shift_one = first_back(grad_normed_one)
    grad_inputs = (grad_hidden + grad_layer_in).reshape(sequence_count, length, width)
    branch_parts = (
        lax.psum_scatter(
            grad_expand.astype(jnp.bfloat16), "shard", scatter_dimension=0, tiled=True
        ).astype(jnp.float32),
        lax.psum_scatter(
            grad_expand_shift.astype(jnp.bfloat16), "shard", scatter_dimension=0, tiled=True
        ).astype(jnp.float32),
        lax.psum_scatter(
            grad_contract.astype(jnp.bfloat16), "shard", scatter_dimension=0, tiled=True
        ).astype(jnp.float32),
        lax.psum_scatter(
            grad_contract_shift.astype(jnp.bfloat16), "shard", scatter_dimension=0, tiled=True
        ).astype(jnp.float32),
        lax.psum_scatter(
            grad_gain_two.astype(jnp.bfloat16), "shard", scatter_dimension=0, tiled=True
        ).astype(jnp.float32),
        lax.psum_scatter(
            grad_shift_two.astype(jnp.bfloat16), "shard", scatter_dimension=0, tiled=True
        ).astype(jnp.float32),
    )
    mixer_parts = (
        lax.psum_scatter(
            grad_query.astype(jnp.bfloat16), "shard", scatter_dimension=0, tiled=True
        ).astype(jnp.float32),
        lax.psum_scatter(
            grad_key.astype(jnp.bfloat16), "shard", scatter_dimension=0, tiled=True
        ).astype(jnp.float32),
        lax.psum_scatter(
            grad_value.astype(jnp.bfloat16), "shard", scatter_dimension=0, tiled=True
        ).astype(jnp.float32),
        lax.psum_scatter(
            grad_control_full.astype(jnp.bfloat16), "shard", scatter_dimension=0, tiled=True
        ).astype(jnp.float32),
        lax.psum_scatter(
            grad_output.astype(jnp.bfloat16), "shard", scatter_dimension=0, tiled=True
        ).astype(jnp.float32),
        lax.psum_scatter(
            grad_gain_one.astype(jnp.bfloat16), "shard", scatter_dimension=0, tiled=True
        ).astype(jnp.float32),
        lax.psum_scatter(
            grad_shift_one.astype(jnp.bfloat16), "shard", scatter_dimension=0, tiled=True
        ).astype(jnp.float32),
    )
    (
        part_expand,
        part_expand_shift,
        part_contract,
        part_contract_shift,
        part_gain_two,
        part_shift_two,
    ) = branch_parts
    part_query, part_key, part_value, part_control, part_output, part_gain_one, part_shift_one = (
        mixer_parts
    )
    summed = (
        lax.psum(part_query.astype(jnp.bfloat16), "rep").astype(jnp.float32),
        lax.psum(part_key.astype(jnp.bfloat16), "rep").astype(jnp.float32),
        lax.psum(part_value.astype(jnp.bfloat16), "rep").astype(jnp.float32),
        lax.psum(part_control.astype(jnp.bfloat16), "rep").astype(jnp.float32),
        lax.psum(part_output.astype(jnp.bfloat16), "rep").astype(jnp.float32),
        lax.psum(part_gain_one.astype(jnp.bfloat16), "rep").astype(jnp.float32),
        lax.psum(part_shift_one.astype(jnp.bfloat16), "rep").astype(jnp.float32),
        lax.psum(part_expand.astype(jnp.bfloat16), "rep").astype(jnp.float32),
        lax.psum(part_expand_shift.astype(jnp.bfloat16), "rep").astype(jnp.float32),
        lax.psum(part_contract.astype(jnp.bfloat16), "rep").astype(jnp.float32),
        lax.psum(part_contract_shift.astype(jnp.bfloat16), "rep").astype(jnp.float32),
        lax.psum(part_gain_two.astype(jnp.bfloat16), "rep").astype(jnp.float32),
        lax.psum(part_shift_two.astype(jnp.bfloat16), "rep").astype(jnp.float32),
    )
    return (
        layer_out,
        grad_inputs,
        loss_value,
        summed[0],
        summed[1],
        summed[2],
        summed[3],
        summed[4],
        summed[5],
        summed[6],
        summed[7],
        summed[8],
        summed[9],
        summed[10],
        summed[11],
        summed[12],
    )


def solution(mesh):
    in_specs = (
        P(("rep", "shard"), None, None),
        P(("rep", "shard"), None),
        P(("rep", "shard"), None),
        P(("rep", "shard"), None, None),
        P("shard", None),
        P("shard", None),
        P("shard", None),
        P("shard", None),
        P("shard", None),
        P("shard"),
        P("shard"),
        P("shard", None),
        P("shard"),
        P("shard", None),
        P("shard"),
        P("shard"),
        P("shard"),
    )
    out_specs = (
        P(("rep", "shard"), None, None),
        P(("rep", "shard"), None, None),
        P(),
        P("shard", None),
        P("shard", None),
        P("shard", None),
        P("shard", None),
        P("shard", None),
        P("shard"),
        P("shard"),
        P("shard", None),
        P("shard"),
        P("shard", None),
        P("shard"),
        P("shard"),
        P("shard"),
    )
    return jax.shard_map(local, mesh=mesh, in_specs=in_specs, out_specs=out_specs, check_vma=False)
```

profile of v0, /device:TPU:0, one launch (start us, length us, event | category | flops | bytes accessed | tf_op | source)
XLA Modules:
  0.0 1280.8 jit_solution(18241503229063410139)
XLA Ops:
  15.0 23.7 %all-reduce.13 = (bf16[512]{0:T(512)(128)(2,1)S(1)}, bf16[512]{0:T(512)(128)(2,1)S(1)}, bf16[512]{0:T(512)(128)(2,1)S(1)}, bf16[512]{0:T(512)(128)(2,1)S(1)}, bf16[512]{0:T(512)(128)(2,1)S(1)}) all-reduce(bf16[512]{0:T(512)(128)(2,1)S(1)} %dynamic-update-slice.1, ...), channel_id=1, replica_groups=mesh['rep'=4,'shard'=8] {'shard'}, use_global_device_ids=true, to_apply=%add.1 | all-reduce | flops 2560 | bytes 10240
  38.7 33.0 %all_gather.48 = bf16[512,512]{1,0:T(8,128)(2,1)S(1)} all-gather(bf16[64,512]{1,0:T(8,128)(2,1)} %param.25), channel_id=1, replica_groups=mesh['rep'=4,'shard'=8] {'shard'}, dimensions={0}, use_global_device_ids=true | all-gather | bytes 589824 | tf_op jit(solution)/shard_map/all_gather | solution.py:114
  71.7 32.5 %all_gather.49 = bf16[512,512]{1,0:T(8,128)(2,1)S(1)} all-gather(bf16[64,512]{1,0:T(8,128)(2,1)} %param.26), channel_id=1, replica_groups=mesh['rep'=4,'shard'=8] {'shard'}, dimensions={0}, use_global_device_ids=true | all-gather | bytes 589824 | tf_op jit(solution)/shard_map/all_gather | solution.py:115
  104.3 32.6 %all_gather.51 = bf16[512,512]{1,0:T(8,128)(2,1)S(1)} all-gather(bf16[64,512]{1,0:T(8,128)(2,1)} %param.27), channel_id=1, replica_groups=mesh['rep'=4,'shard'=8] {'shard'}, dimensions={0}, use_global_device_ids=true | all-gather | bytes 589824 | tf_op jit(solution)/shard_map/all_gather | solution.py:116
  136.8 31.2 %all_gather.50 = bf16[512,512]{1,0:T(8,128)(2,1)S(1)} all-gather(bf16[64,512]{1,0:T(8,128)(2,1)S(1)} %copy-done.27), channel_id=1, replica_groups=mesh['rep'=4,'shard'=8] {'shard'}, dimensions={0}, use_global_device_ids=true | all-gather | bytes 589824 | tf_op jit(solution)/shard_map/all_gather | solution.py:117
  185.8 126.4 %while.48 = (s32[]{:T(128)}, bf16[8,1024,64]{1,2,0:T(8,128)(2,1)S(1)}, bf16[8,1024,64]{2,1,0:T(8,128)(2,1)}, bf16[8,1024,64]{2,1,0:T(8,128)(2,1)}, f32[8,1024,64...) while((s32[]{:T(128)}, bf16[8,1024,64]{1,2,0:T(8,128)(2,1)S(1)}, ...), condition=%wide.region_5.6_spmd.clone, body=%wide.region_2.5_spmd.clone.sunk | while | flops 2571565056 | bytes 21272672 | solution.py:69
  190.7 4.9 fusion.317
  206.5 4.9 fusion.317
  222.2 4.9 fusion.317
  238.0 4.9 fusion.317
  253.7 4.9 fusion.317
  269.4 4.9 fusion.317
  285.2 4.9 fusion.317
  300.9 4.9 fusion.317
  312.3 16.9 %all-gather = bf16[8,1,256]{2,1,0:T(2,128)(2,1)S(1)} all-gather(bf16[1,1,256]{2,1,0:T(2,128)(2,1)S(1)} %reshape.342), channel_id=1, replica_groups=mesh['rep'=4,'shard'=8] {'shard'}, dimensions={0}, use_global_device_ids=true | all-gather | bytes 4608 | tf_op jit(solution)/shard_map/all_gather | solution.py:141
  332.1 31.3 %all_gather.52 = bf16[512,512]{1,0:T(8,128)(2,1)S(1)} all-gather(bf16[64,512]{1,0:T(8,128)(2,1)S(1)} %copy-done.28), channel_id=1, replica_groups=mesh['rep'=4,'shard'=8] {'shard'}, dimensions={0}, use_global_device_ids=true | all-gather | bytes 589824 | tf_op jit(solution)/shard_map/all_gather | solution.py:118
  366.0 7.4 fusion.220
  373.4 8.4 fusion.205
  381.8 37.4 %all-reduce.11 = (f32[]{:T(128)}, f32[]{:T(128)}) all-reduce(f32[]{:T(128)} %convert_reduce_fusion.1, f32[]{:T(128)} %get-tuple-element.343), channel_id=1, replica_groups=mesh['rep'=4,'shard'=8] {'rep','shard'}, use_global_device_ids=true, to_apply=%region_9.10 | all-reduce | flops 2 | bytes 16 | tf_op jit(solution)/shard_map/psum | solution.py:112
  422.7 6.9 fusion.235
  429.6 4.2 fusion.236
  445.8 3.9 fusion.212
  449.7 3.8 copy.61
  458.0 363.5 %while.49 = (s32[]{:T(128)}, bf16[8,1024,64]{1,2,0:T(8,128)(2,1)}, bf16[8,1024,64]{1,2,0:T(8,128)(2,1)}, bf16[8,1024,64]{1,2,0:T(8,128)(2,1)}, bf16[8,1024,64]{1...) while((s32[]{:T(128)}, bf16[8,1024,64]{1,2,0:T(8,128)(2,1)}, ...), condition=%wide.region_16.17_spmd.clone, body=%wide.region_12.16_spmd.clone.sunk | while | flops 7448756224 | bytes 66475184 | solution.py:75
  483.8 4.8 fusion.336
  488.7 4.7 multiply_reduce_fusion.5
  498.1 4.0 fusion.347
  505.7 3.6 fusion.344
  525.7 4.8 fusion.336
  530.6 4.7 multiply_reduce_fusion.5
  540.0 4.0 fusion.347
  547.6 3.6 fusion.344
  567.5 4.8 fusion.336
  572.5 4.7 multiply_reduce_fusion.5
  581.9 4.0 fusion.347
  589.5 3.6 fusion.344
  609.4 4.8 fusion.336
  614.3 4.7 multiply_reduce_fusion.5
  623.8 4.0 fusion.347
  651.3 4.8 fusion.336
  656.2 4.7 multiply_reduce_fusion.5
  665.7 4.0 fusion.347
  693.2 4.8 fusion.336
  698.1 4.7 multiply_reduce_fusion.5
  707.6 4.0 fusion.347
  715.1 3.6 fusion.344
  735.0 4.8 fusion.336
  740.0 4.7 multiply_reduce_fusion.5
  749.4 4.0 fusion.347
  757.0 3.6 fusion.344
  776.9 4.8 fusion.336
  781.9 4.7 multiply_reduce_fusion.5
  791.3 4.0 fusion.347
  833.1 7.4 convolution_convert_fusion
  841.1 6.0 convolution_convert_fusion.1
  856.8 31.3 %reduce-scatter.8.cloned.1.call-done = bf16[64,512]{1,0:T(8,128)(2,1)} async-done(((bf16[512,512]{1,0:T(8,128)(2,1)}), bf16[64,512]{1,0:T(8,128)(2,1)}) %reduce-scatter.8.cloned.1.call-update) | async-done | bytes 65552 | tf_op jit(solution)/shard_map/reduce_scatter | solution.py:242
  888.0 64.2 %reduce-scatter.14.cloned.1.call-done = bf16[64,512]{1,0:T(8,128)(2,1)} async-done(((bf16[512,512]{1,0:T(8,128)(2,1)}), bf16[64,512]{1,0:T(8,128)(2,1)}) %reduce-scatter.14.cloned.1.call-update) | async-done | bytes 65552 | tf_op jit(solution)/shard_map/reduce_scatter | solution.py:251
  952.2 64.5 %reduce-scatter.10.cloned.1.call-done = bf16[64,512]{1,0:T(8,128)(2,1)} async-done(((bf16[512,512]{1,0:T(8,128)(2,1)}), bf16[64,512]{1,0:T(8,128)(2,1)}) %reduce-scatter.10.cloned.1.call-update) | async-done | bytes 65552 | tf_op jit(solution)/shard_map/reduce_scatter | solution.py:245
  1016.7 64.3 %reduce-scatter.12.cloned.1.call-done = bf16[64,512]{1,0:T(8,128)(2,1)} async-done(((bf16[512,512]{1,0:T(8,128)(2,1)}), bf16[64,512]{1,0:T(8,128)(2,1)}) %reduce-scatter.12.cloned.1.call-update) | async-done | bytes 65552 | tf_op jit(solution)/shard_map/reduce_scatter | solution.py:248
  1081.0 70.8 %reduce-scatter.20.cloned.1.call-done = bf16[256,512]{1,0:T(8,128)(2,1)} async-done(((bf16[2048,512]{1,0:T(8,128)(2,1)}), bf16[256,512]{1,0:T(8,128)(2,1)}) %reduce-scatter.20.cloned.1.call-update) | async-done | bytes 262160 | tf_op jit(solution)/shard_map/reduce_scatter | solution.py:228
  1151.8 70.7 %reduce-scatter.18.cloned.1.call-done = bf16[64,2048]{1,0:T(8,128)(2,1)} async-done(((bf16[512,2048]{1,0:T(8,128)(2,1)}), bf16[64,2048]{1,0:T(8,128)(2,1)}) %reduce-scatter.18.cloned.1.call-update) | async-done | bytes 262160 | tf_op jit(solution)/shard_map/reduce_scatter | solution.py:222
  1225.5 19.6 %all-reduce.12 = (bf16[512]{0:T(512)(128)(2,1)S(1)}, bf16[512]{0:T(512)(128)(2,1)S(1)}, bf16[2048]{0:T(1024)(128)(2,1)S(1)}, bf16[512]{0:T(512)(128)(2,1)S(1)}, ...) all-reduce(bf16[512]{0:T(512)(128)(2,1)S(1)} %get-tuple-element.262, ...), channel_id=7, replica_groups=mesh['rep'=4,'shard'=8] {'shard'}, use_global_device_ids=true, to_apply=%region_32.33.clone | all-reduce | flops 4608 | bytes 18432
  1245.6 5.6 all-reduce.14
  1254.3 3.6 add_bitcast_fusion
  (383 shorter events, 382.8 us)
Async XLA Ops:
  7.2 129.6 %copy-start.27 = (bf16[64,512]{1,0:T(8,128)(2,1)S(1)}, bf16[64,512]{1,0:T(8,128)(2,1)}, u32[]{:S(2)}) copy-start(bf16[64,512]{1,0:T(8,128)(2,1)} %param.28) | copy-start | bytes 196612
  7.2 358.8 %all-gather.4.cloned.1.call-start = ((), (), s32[]{:S(2)}) async-start(), calls=%async_computation.7 | async-start | bytes 2359296 | tf_op jit(solution)/shard_map/all_gather | solution.py:140
  7.9 365.5 %all-gather.6.cloned.1.call-start = ((), (), s32[]{:S(2)}) async-start(), calls=%async_computation.8 | async-start | bytes 2359296 | tf_op jit(solution)/shard_map/all_gather | solution.py:142
  8.7 848.1 %reduce-scatter.16.cloned.1.call-start = ((), (), s32[]{:S(2)}) async-start(), calls=%async_computation.13 | async-start | bytes 589824 | tf_op jit(solution)/shard_map/reduce_scatter | solution.py:254
  38.7 144.7 %copy-start.39 = (f32[512]{0:T(512)}, f32[512]{0:T(512)S(1)}, u32[]{:S(2)}) copy-start(f32[512]{0:T(512)S(1)} %convert_element_type.286) | copy-start | bytes 6148
  38.7 144.7 %copy-start.33 = (f32[512]{0:T(512)}, f32[512]{0:T(512)S(1)}, u32[]{:S(2)}) copy-start(f32[512]{0:T(512)S(1)} %convert_element_type.285) | copy-start | bytes 6148
  71.7 109.0 %copy-start.23 = (bf16[512,512]{1,0:T(8,128)(2,1)}, bf16[512,512]{1,0:T(8,128)(2,1)S(1)}, u32[]{:S(2)}) copy-start(bf16[512,512]{1,0:T(8,128)(2,1)S(1)} %all_gather.48) | copy-start | bytes 1572868
  104.2 67.4 %copy-start.19 = (bf16[512,512]{1,0:T(8,128)(2,1)}, bf16[512,512]{1,0:T(8,128)(2,1)S(1)}, u32[]{:S(2)}) copy-start(bf16[512,512]{1,0:T(8,128)(2,1)S(1)} %all_gather.49) | copy-start | bytes 1572868
  136.8 39.4 %copy-start.21 = (bf16[512,512]{1,0:T(8,128)(2,1)}, bf16[512,512]{1,0:T(8,128)(2,1)S(1)}, u32[]{:S(2)}) copy-start(bf16[512,512]{1,0:T(8,128)(2,1)S(1)} %all_gather.51) | copy-start | bytes 1572868
  168.0 0.8 copy-start.12
  170.5 192.9 %copy-start = (bf16[1,1024,512]{1,2,0:T(8,128)(2,1)}, bf16[1,1024,512]{1,2,0:T(8,128)(2,1)S(1)}, u32[]{:S(2)}) copy-start(bf16[1,1024,512]{1,2,0:T(8,128)(2,1)S(1)} %copy.51) | copy-start | bytes 3145732
  170.7 12.7 copy-start.25
  171.6 11.8 copy-start.29
  183.4 2.3 copy-start.46
  185.8 126.4 %copy-start.47 = (bf16[256]{0:T(256)(128)(2,1)S(1)}, bf16[256]{0:T(256)(128)(2,1)}, u32[]{:S(2)}) copy-start(bf16[256]{0:T(256)(128)(2,1)} %param.33) | copy-start | bytes 1540
  185.8 126.5 %copy-start.35 = (s32[1,1024]{1,0:T(1,128)S(1)}, s32[1,1024]{1,0:T(1,128)}, u32[]{:S(2)}) copy-start(s32[1,1024]{1,0:T(1,128)} %param.23) | copy-start | bytes 12292
  312.2 51.2 %copy-start.6 = (bf16[8,1024,64]{1,2,0:T(8,128)(2,1)}, bf16[8,1024,64]{1,2,0:T(8,128)(2,1)S(1)}, u32[]{:S(2)}) copy-start(bf16[8,1024,64]{1,2,0:T(8,128)(2,1)S(1)} %get-tuple-element.167) | copy-start | bytes 3145732
  312.2 19.9 %copy-start.28 = (bf16[64,512]{1,0:T(8,128)(2,1)S(1)}, bf16[64,512]{1,0:T(8,128)(2,1)}, u32[]{:S(2)}) copy-start(bf16[64,512]{1,0:T(8,128)(2,1)} %param.29) | copy-start | bytes 196612
  312.2 53.7 %copy-start.41 = (f32[512]{0:T(512)}, f32[512]{0:T(512)S(1)}, u32[]{:S(2)}) copy-start(f32[512]{0:T(512)S(1)} %convert_element_type.298) | copy-start | bytes 6148
  363.4 2.2 copy-start.14
  365.9 7.5 copy-start.8
  420.0 2.7 copy-start.45
  422.7 7.0 copy-start.24
  422.7 7.0 copy-start.44
  429.6 4.2 copy-start.48
  436.8 2.2 copy-start.4
  439.0 1.4 copy-start.9
  439.0 1.9 copy-start.10
  440.9 3.3 copy-start.7
  442.9 1.3 copy-start.2
  449.7 438.3 %reduce-scatter.8.cloned.1.call-start = ((), (), s32[]{:S(2)}) async-start(), calls=%async_computation.9 | async-start | bytes 589824 | tf_op jit(solution)/shard_map/reduce_scatter | solution.py:242
  458.0 363.6 %copy-start.1 = (bf16[1,1024,512]{1,2,0:T(8,128)(2,1)S(1)}, bf16[1,1024,512]{1,2,0:T(8,128)(2,1)}, u32[]{:S(2)}) copy-start(bf16[1,1024,512]{1,2,0:T(8,128)(2,1)} %copy-done) | copy-start | bytes 3145732
  458.0 363.6 %copy-start.26 = (f32[1024]{0:T(1024)S(1)}, f32[1024]{0:T(1024)}, u32[]{:S(2)}) copy-start(f32[1024]{0:T(1024)} %copy-done.25) | copy-start | bytes 12292
  458.0 363.6 %copy-start.30 = (f32[1024]{0:T(1024)S(1)}, f32[1024]{0:T(1024)}, u32[]{:S(2)}) copy-start(f32[1024]{0:T(1024)} %copy-done.29) | copy-start | bytes 12292
  458.0 363.6 %copy-start.34 = (f32[512]{0:T(512)S(1)}, f32[512]{0:T(512)}, u32[]{:S(2)}) copy-start(f32[512]{0:T(512)} %copy-done.33) | copy-start | bytes 6148
  458.0 363.6 %copy-start.40 = (f32[512]{0:T(512)S(1)}, f32[512]{0:T(512)}, u32[]{:S(2)}) copy-start(f32[512]{0:T(512)} %copy-done.39) | copy-start | bytes 6148
  481.8 1.9 copy-start.11
  523.7 1.9 copy-start.11
  565.6 1.9 copy-start.11
  607.5 1.9 copy-start.11
  649.4 1.9 copy-start.11
  691.3 1.9 copy-start.11
  733.1 1.9 copy-start.11
  775.0 1.9 copy-start.11
  824.4 127.8 %reduce-scatter.14.cloned.1.call-start = ((), (), s32[]{:S(2)}) async-start(), calls=%async_computation.12 | async-start | bytes 589824 | tf_op jit(solution)/shard_map/reduce_scatter | solution.py:251
  827.3 189.4 %reduce-scatter.10.cloned.1.call-start = ((), (), s32[]{:S(2)}) async-start(), calls=%async_computation.10 | async-start | bytes 589824 | tf_op jit(solution)/shard_map/reduce_scatter | solution.py:245
  830.2 250.8 %reduce-scatter.12.cloned.1.call-start = ((), (), s32[]{:S(2)}) async-start(), calls=%async_computation.11 | async-start | bytes 589824 | tf_op jit(solution)/shard_map/reduce_scatter | solution.py:248
  833.1 318.7 %reduce-scatter.20.cloned.1.call-start = ((), (), s32[]{:S(2)}) async-start(), calls=%async_computation.15 | async-start | bytes 2359296 | tf_op jit(solution)/shard_map/reduce_scatter | solution.py:228
  840.5 382.0 %reduce-scatter.18.cloned.1.call-start = ((), (), s32[]{:S(2)}) async-start(), calls=%async_computation.14 | async-start | bytes 2359296 | tf_op jit(solution)/shard_map/reduce_scatter | solution.py:222
  847.1 1.5 copy-start.17
  847.2 3.3 copy-start.15
  847.2 414.3 %all-reduce.18.cloned.1.call-start = ((), (), s32[]{:S(2)}) async-start(), calls=%async_computation.16 | async-start | bytes 1703936 | tf_op jit(solution)/shard_map/psum | solution.py:276
  848.7 1.8 copy-start.22
  850.5 1.2 copy-start.16
  850.5 1.4 copy-start.20
  851.9 1.0 copy-start.13
  851.9 1.4 copy-start.18
  853.3 1.2 copy-start.32
  854.5 1.3 copy-start.5
  856.7 368.8 %copy-start.36 = (bf16[512]{0:T(512)(128)(2,1)S(1)}, bf16[512]{0:T(512)(128)(2,1)}, u32[]{:S(2)}) copy-start(bf16[512]{0:T(512)(128)(2,1)} %get-tuple-element.260) | copy-start | bytes 3076
  856.7 368.8 %copy-start.37 = (bf16[2048]{0:T(1024)(128)(2,1)S(1)}, bf16[2048]{0:T(1024)(128)(2,1)}, u32[]{:S(2)}) copy-start(bf16[2048]{0:T(1024)(128)(2,1)} %get-tuple-element.346) | copy-start | bytes 12292
  856.7 368.8 %copy-start.38 = (bf16[512]{0:T(512)(128)(2,1)S(1)}, bf16[512]{0:T(512)(128)(2,1)}, u32[]{:S(2)}) copy-start(bf16[512]{0:T(512)(128)(2,1)} %get-tuple-element.330) | copy-start | bytes 3076
  856.7 368.8 %copy-start.43 = (bf16[512]{0:T(512)(128)(2,1)S(1)}, bf16[512]{0:T(512)(128)(2,1)}, u32[]{:S(2)}) copy-start(bf16[512]{0:T(512)(128)(2,1)} %get-tuple-element.348) | copy-start | bytes 3076
  856.7 397.6 %copy-start.3 = (f32[1024,512]{0,1:T(8,128)S(1)}, f32[1024,512]{0,1:T(8,128)}, u32[]{:S(2)}) copy-start(f32[1024,512]{0,1:T(8,128)} %copy-done.2) | copy-start | bytes 6291460
  (2 other events, 1.2 us)
Sparse Core Ops, SparseCore 0:
  10.1 59.2 all-gather.3
  71.6 55.8 all-gather.5
  449.8 63.3 reduce-scatter.15
  824.5 63.4 reduce-scatter.7
  891.2 60.9 reduce-scatter.13
  955.7 60.9 reduce-scatter.9
  1020.0 60.8 reduce-scatter.11
  1084.9 66.8 reduce-scatter.19
  1155.7 66.7 reduce-scatter.17
  1225.5 34.6 all-reduce.17
where the time goes:
time: 1290 us; the launch traced here: 1280 us
  matrix products  519 us (40%)
  waiting for transfers between devices  367 us (28%)
  blocking collectives  264 us (20%)
  local copies, waits for them, and re-layouts  49.7 us (4%)
  other arithmetic  30.4 us (2%)
  loops' own time  30.1 us (2%)
  between operations  20.2 us (2%)
    dot_general x32, matrix products, slot_rest(): slot_scores = jnp.dot(scores * causal, weights, precision=HIGHEST) / totals  134 us
    dot_general x32, matrix products, slot_rest(): jnp.dot(slot_shares / totals, weights.T, precision=HIGHEST) * causal  127 us
    dot_general x37, matrix products, product(): return jnp.dot(left, right, preferred_element_type=jnp.float32)  99.4 us
    reduce_scatter x1, waiting for transfers between devices, local(): lax.psum_scatter(grad_contract.astype(jnp.bfloat16), 'shard', scatter_dim...  70.8 us
    reduce_scatter x1, waiting for transfers between devices, local(): lax.psum_scatter(grad_expand.astype(jnp.bfloat16), 'shard', scatter_dimen...  70.7 us
    dot_general x24, matrix products, slot_rest(): jnp.dot(mixing, value_rows, precision=THREEPASS, preferred_element_type=j...  69.2 us
    reduce_scatter x1, waiting for transfers between devices, local(): lax.psum_scatter(grad_key.astype(jnp.bfloat16), 'shard', scatter_dimensio...  64.5 us
    reduce_scatter x1, waiting for transfers between devices, local(): lax.psum_scatter(grad_value.astype(jnp.bfloat16), 'shard', scatter_dimens...  64.3 us
  transfers between devices with their start and end apart: 10, of which 6 were waited for; matrix products, arithmetic and copies ran while one was open for 43% of the time, Pallas kernels for 0%

commit v1 on v0

--- a/solution.py
+++ b/solution.py
@@ -105,6 +105,22 @@
     gain_second,
     shift_second,
 ):
+
+    def play_unit(m, across):
+        full_n = lax.psum(1, across)
+        blocks_here = [(i0, (i0 + 1) % full_n) for i0 in range(full_n)]
+        buffer = [(i0, (i0 - 1) % full_n) for i0 in range(full_n)]
+        tall, f_now = ([m], [m])
+        for _ in range(full_n // 2):
+            frame_out = lax.ppermute(tall[-1], across, perm=blocks_here)
+            tall.append(frame_out)
+        for _ in range((full_n - 1) // 2):
+            response = lax.ppermute(f_now[-1], across, buffer)
+            f_now.append(response)
+        placed = jnp.concatenate([*tall[::-1], *f_now[1:]], axis=0)
+        row_out = lax.axis_index(across)
+        return jnp.roll(placed, shift=(row_out - full_n // 2) * m.shape[0], axis=0)
+
     sequence_count, length, width = inputs.shape
     total_rows = sequence_count * length
     valid_rows = valid_mask.reshape(total_rows, 1).astype(jnp.float32)
@@ -115,7 +131,7 @@
         lax.all_gather(key_weight, "shard", axis=0, tiled=True),
         lax.all_gather(value_weight, "shard", axis=0, tiled=True),
         lax.all_gather(control_weight, "shard", axis=0, tiled=True),
-        lax.all_gather(output_weight, "shard", axis=0, tiled=True),
+        play_unit(output_weight, "shard"),
         lax.all_gather(gain_first, "shard", axis=0, tiled=True),
         lax.all_gather(shift_first, "shard", axis=0, tiled=True),
     )

time: 1290 us -> 1310 us (1.016)
  transfers between devices with their start and end apart: 10 -> 17, of which waited for: 6 -> 9; matrix products, arithmetic and copies ran while one was open for 43% -> 42% of each run, Pallas kernels for 0% -> 0%
where the time goes in v1:
time: 1310 us; the launch traced here: 1300 us
  matrix products  520 us (40%)
  waiting for transfers between devices  369 us (28%)
  blocking collectives  271 us (21%)
  local copies, waits for them, and re-layouts  48.7 us (4%)
  other arithmetic  30.4 us (2%)
  loops' own time  29.7 us (2%)
  between operations  20.3 us (2%)
    dot_general x32, matrix products, slot_rest(): slot_scores = jnp.dot(scores * causal, weights, precision=HIGHEST) / totals  134 us
    dot_general x32, matrix products, slot_rest(): jnp.dot(slot_shares / totals, weights.T, precision=HIGHEST) * causal  127 us
    dot_general x37, matrix products, product(): return jnp.dot(left, right, preferred_element_type=jnp.float32)  99.9 us
    reduce_scatter x1, waiting for transfers between devices, local(): lax.psum_scatter(grad_contract.astype(jnp.bfloat16), 'shard', scatter_dim...  70.6 us
    reduce_scatter x1, waiting for transfers between devices, local(): lax.psum_scatter(grad_expand.astype(jnp.bfloat16), 'shard', scatter_dimen...  70.6 us
    dot_general x24, matrix products, slot_rest(): jnp.dot(mixing, value_rows, precision=THREEPASS, preferred_element_type=j...  69.2 us
    reduce_scatter x1, waiting for transfers between devices, local(): lax.psum_scatter(grad_key.astype(jnp.bfloat16), 'shard', scatter_dimensio...  64.5 us
    reduce_scatter x1, waiting for transfers between devices, local(): lax.psum_scatter(grad_value.astype(jnp.bfloat16), 'shard', scatter_dimens...  64.3 us
  transfers between devices with their start and end apart: 17, of which 9 were waited for; matrix products, arithmetic and copies ran while one was open for 42% of the time, Pallas kernels for 0%

profile of v1, /device:TPU:0, one launch (start us, length us, event | category | flops | bytes accessed | tf_op | source)
XLA Modules:
  0.0 1301.4 jit_solution(3576006452956139288)
XLA Ops:
  8.0 6.1 collective-permute-start.4
  20.4 22.2 %all-reduce.13 = (bf16[512]{0:T(512)(128)(2,1)S(1)}, bf16[512]{0:T(512)(128)(2,1)S(1)}, bf16[512]{0:T(512)(128)(2,1)S(1)}, bf16[512]{0:T(512)(128)(2,1)S(1)}, bf16[512]{0:T(512)(128)(2,1)S(1)}) all-reduce(bf16[512]{0:T(512)(128)(2,1)S(1)} %dynamic-update-slice.1, ...), channel_id=1, replica_groups=mesh['rep'=4,'shard'=8] {'shard'}, use_global_device_ids=true, to_apply=%add.1 | all-reduce | flops 2560 | bytes 10240
  42.6 32.8 %all_gather.47 = bf16[512,512]{1,0:T(8,128)(2,1)S(1)} all-gather(bf16[64,512]{1,0:T(8,128)(2,1)} %param.25), channel_id=1, replica_groups=mesh['rep'=4,'shard'=8] {'shard'}, dimensions={0}, use_global_device_ids=true | all-gather | bytes 589824 | tf_op jit(solution)/shard_map/all_gather | solution.py:130
  75.4 33.2 %all_gather.48 = bf16[512,512]{1,0:T(8,128)(2,1)S(1)} all-gather(bf16[64,512]{1,0:T(8,128)(2,1)} %param.26), channel_id=1, replica_groups=mesh['rep'=4,'shard'=8] {'shard'}, dimensions={0}, use_global_device_ids=true | all-gather | bytes 589824 | tf_op jit(solution)/shard_map/all_gather | solution.py:131
  108.6 32.3 %all_gather.50 = bf16[512,512]{1,0:T(8,128)(2,1)S(1)} all-gather(bf16[64,512]{1,0:T(8,128)(2,1)} %param.27), channel_id=1, replica_groups=mesh['rep'=4,'shard'=8] {'shard'}, dimensions={0}, use_global_device_ids=true | all-gather | bytes 589824 | tf_op jit(solution)/shard_map/all_gather | solution.py:132
  140.8 31.2 %all_gather.49 = bf16[512,512]{1,0:T(8,128)(2,1)S(1)} all-gather(bf16[64,512]{1,0:T(8,128)(2,1)S(1)} %copy-done.29), channel_id=1, replica_groups=mesh['rep'=4,'shard'=8] {'shard'}, dimensions={0}, use_global_device_ids=true | all-gather | bytes 589824 | tf_op jit(solution)/shard_map/all_gather | solution.py:133
  190.4 126.0 %while.48 = (s32[]{:T(128)}, bf16[8,1024,64]{1,2,0:T(8,128)(2,1)S(1)}, bf16[8,1024,64]{2,1,0:T(8,128)(2,1)}, bf16[8,1024,64]{2,1,0:T(8,128)(2,1)}, f32[8,1024,64...) while((s32[]{:T(128)}, bf16[8,1024,64]{1,2,0:T(8,128)(2,1)S(1)}, ...), condition=%wide.region_5.6_spmd.clone, body=%wide.region_2.5_spmd.clone.sunk | while | flops 2571565056 | bytes 21272672 | solution.py:69
  194.9 5.0 fusion.318
  210.6 5.0 fusion.318
  226.4 5.0 fusion.318
  242.1 5.0 fusion.318
  257.9 5.0 fusion.318
  273.6 5.0 fusion.318
  289.4 5.0 fusion.318
  305.1 5.0 fusion.318
  317.0 34.6 %all_gather.57 = bf16[512,512]{1,0:T(8,128)(2,1)} all-gather(bf16[64,512]{1,0:T(8,128)(2,1)S(1)} %copy-done.26), channel_id=1, replica_groups=mesh['rep'=4,'shard'=8] {'shard'}, dimensions={0}, use_global_device_ids=true | all-gather | bytes 589824 | tf_op jit(solution)/shard_map/all_gather | solution.py:202
  351.7 19.0 %all-gather = bf16[8,1,256]{2,1,0:T(2,128)(2,1)S(1)} all-gather(bf16[1,1,256]{2,1,0:T(2,128)(2,1)S(1)} %reshape.342), channel_id=1, replica_groups=mesh['rep'=4,'shard'=8] {'shard'}, dimensions={0}, use_global_device_ids=true | all-gather | bytes 4608 | tf_op jit(solution)/shard_map/all_gather | solution.py:157
  384.5 7.4 fusion.222
  392.0 8.4 fusion.205
  400.4 40.7 %all-reduce.11 = (f32[]{:T(128)}, f32[]{:T(128)}) all-reduce(f32[]{:T(128)} %convert_reduce_fusion.1, f32[]{:T(128)} %get-tuple-element.343), channel_id=1, replica_groups=mesh['rep'=4,'shard'=8] {'rep','shard'}, use_global_device_ids=true, to_apply=%region_9.10 | all-reduce | flops 2 | bytes 16 | tf_op jit(solution)/shard_map/psum | solution.py:128
  444.5 6.9 fusion.237
  451.5 4.2 fusion.238
  467.4 3.7 fusion.212
  471.1 3.8 copy.61
  479.3 363.8 %while.49 = (s32[]{:T(128)}, bf16[8,1024,64]{1,2,0:T(8,128)(2,1)}, bf16[8,1024,64]{1,2,0:T(8,128)(2,1)}, bf16[8,1024,64]{1,2,0:T(8,128)(2,1)}, bf16[8,1024,64]{1...) while((s32[]{:T(128)}, bf16[8,1024,64]{1,2,0:T(8,128)(2,1)}, ...), condition=%wide.region_16.17_spmd.clone, body=%wide.region_12.16_spmd.clone.sunk | while | flops 7448756224 | bytes 66475184 | solution.py:75
  505.1 4.8 fusion.337
  510.0 4.8 multiply_reduce_fusion.5
  519.5 4.0 fusion.348
  527.0 3.6 fusion.345
  547.0 4.8 fusion.337
  551.9 4.8 multiply_reduce_fusion.5
  561.4 4.0 fusion.348
  569.0 3.6 fusion.345
  588.9 4.8 fusion.337
  593.8 4.8 multiply_reduce_fusion.5
  603.3 4.0 fusion.348
  630.8 4.8 fusion.337
  635.7 4.8 multiply_reduce_fusion.5
  645.2 4.0 fusion.348
  672.7 4.8 fusion.337
  677.6 4.8 multiply_reduce_fusion.5
  687.1 4.0 fusion.348
  694.7 3.6 fusion.345
  714.6 4.8 fusion.337
  719.6 4.8 multiply_reduce_fusion.5
  729.0 4.0 fusion.348
  756.5 4.8 fusion.337
  761.5 4.8 multiply_reduce_fusion.5
  770.9 4.0 fusion.348
  798.4 4.8 fusion.337
  803.4 4.8 multiply_reduce_fusion.5
  812.8 4.0 fusion.348
  820.4 3.6 fusion.345
  854.7 7.4 convolution_convert_fusion
  862.7 6.0 convolution_convert_fusion.1
  878.3 30.6 %reduce-scatter.8.cloned.1.call-done = bf16[64,512]{1,0:T(8,128)(2,1)} async-done(((bf16[512,512]{1,0:T(8,128)(2,1)}), bf16[64,512]{1,0:T(8,128)(2,1)}) %reduce-scatter.8.cloned.1.call-update) | async-done | bytes 65552 | tf_op jit(solution)/shard_map/reduce_scatter | solution.py:258
  908.9 64.2 %reduce-scatter.14.cloned.1.call-done = bf16[64,512]{1,0:T(8,128)(2,1)} async-done(((bf16[512,512]{1,0:T(8,128)(2,1)}), bf16[64,512]{1,0:T(8,128)(2,1)}) %reduce-scatter.14.cloned.1.call-update) | async-done | bytes 65552 | tf_op jit(solution)/shard_map/reduce_scatter | solution.py:267
  973.1 64.5 %reduce-scatter.10.cloned.1.call-done = bf16[64,512]{1,0:T(8,128)(2,1)} async-done(((bf16[512,512]{1,0:T(8,128)(2,1)}), bf16[64,512]{1,0:T(8,128)(2,1)}) %reduce-scatter.10.cloned.1.call-update) | async-done | bytes 65552 | tf_op jit(solution)/shard_map/reduce_scatter | solution.py:261
  1037.6 64.3 %reduce-scatter.12.cloned.1.call-done = bf16[64,512]{1,0:T(8,128)(2,1)} async-done(((bf16[512,512]{1,0:T(8,128)(2,1)}), bf16[64,512]{1,0:T(8,128)(2,1)}) %reduce-scatter.12.cloned.1.call-update) | async-done | bytes 65552 | tf_op jit(solution)/shard_map/reduce_scatter | solution.py:264
  1101.9 70.6 %reduce-scatter.20.cloned.1.call-done = bf16[256,512]{1,0:T(8,128)(2,1)} async-done(((bf16[2048,512]{1,0:T(8,128)(2,1)}), bf16[256,512]{1,0:T(8,128)(2,1)}) %reduce-scatter.20.cloned.1.call-update) | async-done | bytes 262160 | tf_op jit(solution)/shard_map/reduce_scatter | solution.py:244
  1172.6 70.6 %reduce-scatter.18.cloned.1.call-done = bf16[64,2048]{1,0:T(8,128)(2,1)} async-done(((bf16[512,2048]{1,0:T(8,128)(2,1)}), bf16[64,2048]{1,0:T(8,128)(2,1)}) %reduce-scatter.18.cloned.1.call-update) | async-done | bytes 262160 | tf_op jit(solution)/shard_map/reduce_scatter | solution.py:238
  1246.1 19.6 %all-reduce.12 = (bf16[512]{0:T(512)(128)(2,1)S(1)}, bf16[512]{0:T(512)(128)(2,1)S(1)}, bf16[2048]{0:T(1024)(128)(2,1)S(1)}, bf16[512]{0:T(512)(128)(2,1)S(1)}, ...) all-reduce(bf16[512]{0:T(512)(128)(2,1)S(1)} %get-tuple-element.262, ...), channel_id=7, replica_groups=mesh['rep'=4,'shard'=8] {'shard'}, use_global_device_ids=true, to_apply=%region_32.33.clone | all-reduce | flops 4608 | bytes 18432
  1266.2 5.6 all-reduce.14
  1275.0 3.6 add_bitcast_fusion
  (415 shorter events, 395.1 us)
Async XLA Ops:
  7.2 133.6 %copy-start.29 = (bf16[64,512]{1,0:T(8,128)(2,1)S(1)}, bf16[64,512]{1,0:T(8,128)(2,1)}, u32[]{:S(2)}) copy-start(bf16[64,512]{1,0:T(8,128)(2,1)} %param.28) | copy-start | bytes 196612
  7.2 377.3 %all-gather.4.cloned.1.call-start = ((), (), s32[]{:S(2)}) async-start(), calls=%async_computation.7 | async-start | bytes 2359296 | tf_op jit(solution)/shard_map/all_gather | solution.py:156
  7.9 384.1 %all-gather.6.cloned.1.call-start = ((), (), s32[]{:S(2)}) async-start(), calls=%async_computation.8 | async-start | bytes 2359296 | tf_op jit(solution)/shard_map/all_gather | solution.py:158
  8.0 365.0 %collective-permute-start.4 = (bf16[64,512]{1,0:T(8,128)(2,1)}, bf16[64,512]{1,0:T(8,128)(2,1)S(1)}, u32[]{:S(2)}, u32[]{:S(2)}) collective-permute-start(bf16[64,512]{1,0:T(8,128)(2,1)} %param.29), channel_id=1, source_target_pairs={{0,7},{1,0},{2,1},{3,2},{4,3},{5,4},{6,5},{7,6},{8,15},{9,8},{10,9... | collective-permute-start | bytes 196616 | tf_op jit(solution)/shard_map/ppermute | solution.py:118
  14.0 175.7 %collective-permute-start = (bf16[64,512]{1,0:T(8,128)(2,1)}, bf16[64,512]{1,0:T(8,128)(2,1)S(1)}, u32[]{:S(2)}, u32[]{:S(2)}) collective-permute-start(bf16[64,512]{1,0:T(8,128)(2,1)} %param.29), channel_id=1, source_target_pairs={{0,1},{1,2},{2,3},{3,4},{4,5},{5,6},{6,7},{7,0},{8,9},{9,10},{10,1... | collective-permute-start | bytes 196616 | tf_op jit(solution)/shard_map/ppermute | solution.py:115
  14.1 864.3 %reduce-scatter.16.cloned.1.call-start = ((), (), s32[]{:S(2)}) async-start(), calls=%async_computation.13 | async-start | bytes 589824 | tf_op jit(solution)/shard_map/reduce_scatter | solution.py:270
  42.6 138.9 %copy-start.40 = (f32[512]{0:T(512)}, f32[512]{0:T(512)S(1)}, u32[]{:S(2)}) copy-start(f32[512]{0:T(512)S(1)} %convert_element_type.286) | copy-start | bytes 6148
  42.6 138.9 %copy-start.34 = (f32[512]{0:T(512)}, f32[512]{0:T(512)S(1)}, u32[]{:S(2)}) copy-start(f32[512]{0:T(512)S(1)} %convert_element_type.285) | copy-start | bytes 6148
  75.4 106.2 %copy-start.21 = (bf16[512,512]{1,0:T(8,128)(2,1)}, bf16[512,512]{1,0:T(8,128)(2,1)S(1)}, u32[]{:S(2)}) copy-start(bf16[512,512]{1,0:T(8,128)(2,1)S(1)} %all_gather.47) | copy-start | bytes 1572868
  108.6 67.1 %copy-start.17 = (bf16[512,512]{1,0:T(8,128)(2,1)}, bf16[512,512]{1,0:T(8,128)(2,1)S(1)}, u32[]{:S(2)}) copy-start(bf16[512,512]{1,0:T(8,128)(2,1)S(1)} %all_gather.48) | copy-start | bytes 1572868
  140.8 36.7 %copy-start.19 = (bf16[512,512]{1,0:T(8,128)(2,1)}, bf16[512,512]{1,0:T(8,128)(2,1)S(1)}, u32[]{:S(2)}) copy-start(bf16[512,512]{1,0:T(8,128)(2,1)S(1)} %all_gather.50) | copy-start | bytes 1572868
  174.5 207.7 %copy-start = (bf16[1,1024,512]{1,2,0:T(8,128)(2,1)}, bf16[1,1024,512]{1,2,0:T(8,128)(2,1)S(1)}, u32[]{:S(2)}) copy-start(bf16[1,1024,512]{1,2,0:T(8,128)(2,1)S(1)} %copy.51) | copy-start | bytes 3145732
  174.7 6.8 copy-start.27
  175.6 5.9 copy-start.30
  183.4 2.8 copy-start.23
  186.2 1.8 copy-start.24
  188.0 2.3 copy-start.47
  189.8 126.6 %collective-permute-start.1 = (bf16[64,512]{1,0:T(8,128)(2,1)S(1)}, bf16[64,512]{1,0:T(8,128)(2,1)S(1)}, u32[]{:S(2)}, u32[]{:S(2)}) collective-permute-start(bf16[64,512]{1,0:T(8,128)(2,1)S(1)} %collective-permute-done), channel_id=1, source_target_pairs={{0,1},{1,2},{2,3},{3,4},{4,5},{5,6},{6,7},{7,0},{8,9},{9,10},{10,1... | collective-permute-start | bytes 196616 | tf_op jit(solution)/shard_map/ppermute | solution.py:115
  190.4 126.6 %copy-start.26 = (bf16[64,512]{1,0:T(8,128)(2,1)S(1)}, bf16[64,512]{1,0:T(8,128)(2,1)}, u32[]{:S(2)}) copy-start(bf16[64,512]{1,0:T(8,128)(2,1)} %param.29) | copy-start | bytes 196612
  190.4 161.2 %copy-start.48 = (bf16[256]{0:T(256)(128)(2,1)S(1)}, bf16[256]{0:T(256)(128)(2,1)}, u32[]{:S(2)}) copy-start(bf16[256]{0:T(256)(128)(2,1)} %param.33) | copy-start | bytes 1540
  190.4 161.3 %copy-start.36 = (s32[1,1024]{1,0:T(1,128)S(1)}, s32[1,1024]{1,0:T(1,128)}, u32[]{:S(2)}) copy-start(s32[1,1024]{1,0:T(1,128)} %param.23) | copy-start | bytes 12292
  316.4 65.7 %copy-start.6 = (bf16[8,1024,64]{1,2,0:T(8,128)(2,1)}, bf16[8,1024,64]{1,2,0:T(8,128)(2,1)S(1)}, u32[]{:S(2)}) copy-start(bf16[8,1024,64]{1,2,0:T(8,128)(2,1)S(1)} %get-tuple-element.167) | copy-start | bytes 3145732
  316.4 56.8 %collective-permute-start.2 = (bf16[64,512]{1,0:T(8,128)(2,1)S(1)}, bf16[64,512]{1,0:T(8,128)(2,1)S(1)}, u32[]{:S(2)}, u32[]{:S(2)}) collective-permute-start(bf16[64,512]{1,0:T(8,128)(2,1)S(1)} %collective-permute-done.1), channel_id=1, source_target_pairs={{0,1},{1,2},{2,3},{3,4},{4,5},{5,6},{6,7},{7,0},{8,9},{9,10},{10,1... | collective-permute-start | bytes 196616 | tf_op jit(solution)/shard_map/ppermute | solution.py:115
  351.6 32.9 %copy-start.42 = (f32[512]{0:T(512)}, f32[512]{0:T(512)S(1)}, u32[]{:S(2)}) copy-start(f32[512]{0:T(512)S(1)} %convert_element_type.298) | copy-start | bytes 6148
  373.0 4.5 collective-permute-start.5
  373.2 7.0 collective-permute-start.3
  377.4 4.6 collective-permute-start.6
  384.5 7.5 copy-start.8
  441.8 2.7 copy-start.46
  444.5 7.0 copy-start.25
  444.5 7.0 copy-start.45
  451.5 4.2 copy-start.49
  458.6 2.2 copy-start.4
  460.8 1.6 copy-start.9
  462.4 3.3 copy-start.7
  465.8 1.6 copy-start.22
  467.4 441.6 %reduce-scatter.8.cloned.1.call-start = ((), (), s32[]{:S(2)}) async-start(), calls=%async_computation.9 | async-start | bytes 589824 | tf_op jit(solution)/shard_map/reduce_scatter | solution.py:258
  479.3 363.8 %copy-start.1 = (bf16[1,1024,512]{1,2,0:T(8,128)(2,1)S(1)}, bf16[1,1024,512]{1,2,0:T(8,128)(2,1)}, u32[]{:S(2)}) copy-start(bf16[1,1024,512]{1,2,0:T(8,128)(2,1)} %copy-done) | copy-start | bytes 3145732
  479.3 363.8 %copy-start.28 = (f32[1024]{0:T(1024)S(1)}, f32[1024]{0:T(1024)}, u32[]{:S(2)}) copy-start(f32[1024]{0:T(1024)} %copy-done.27) | copy-start | bytes 12292
  479.3 363.8 %copy-start.31 = (f32[1024]{0:T(1024)S(1)}, f32[1024]{0:T(1024)}, u32[]{:S(2)}) copy-start(f32[1024]{0:T(1024)} %copy-done.30) | copy-start | bytes 12292
  479.3 363.8 %copy-start.35 = (f32[512]{0:T(512)S(1)}, f32[512]{0:T(512)}, u32[]{:S(2)}) copy-start(f32[512]{0:T(512)} %copy-done.34) | copy-start | bytes 6148
  479.3 363.8 %copy-start.41 = (f32[512]{0:T(512)S(1)}, f32[512]{0:T(512)}, u32[]{:S(2)}) copy-start(f32[512]{0:T(512)} %copy-done.40) | copy-start | bytes 6148
  503.2 1.9 copy-start.10
  545.1 1.9 copy-start.10
  587.0 1.9 copy-start.10
  628.9 1.9 copy-start.10
  670.8 1.9 copy-start.10
  712.7 1.9 copy-start.10
  754.6 1.9 copy-start.10
  796.5 1.9 copy-start.10
  846.0 127.1 %reduce-scatter.14.cloned.1.call-start = ((), (), s32[]{:S(2)}) async-start(), calls=%async_computation.12 | async-start | bytes 589824 | tf_op jit(solution)/shard_map/reduce_scatter | solution.py:267
  848.9 188.7 %reduce-scatter.10.cloned.1.call-start = ((), (), s32[]{:S(2)}) async-start(), calls=%async_computation.10 | async-start | bytes 589824 | tf_op jit(solution)/shard_map/reduce_scatter | solution.py:261
  851.7 250.2 %reduce-scatter.12.cloned.1.call-start = ((), (), s32[]{:S(2)}) async-start(), calls=%async_computation.11 | async-start | bytes 589824 | tf_op jit(solution)/shard_map/reduce_scatter | solution.py:264
  854.6 317.9 %reduce-scatter.20.cloned.1.call-start = ((), (), s32[]{:S(2)}) async-start(), calls=%async_computation.15 | async-start | bytes 2359296 | tf_op jit(solution)/shard_map/reduce_scatter | solution.py:244
  862.0 381.1 %reduce-scatter.18.cloned.1.call-start = ((), (), s32[]{:S(2)}) async-start(), calls=%async_computation.14 | async-start | bytes 2359296 | tf_op jit(solution)/shard_map/reduce_scatter | solution.py:238
  868.7 1.5 copy-start.15
  868.7 3.3 copy-start.13
  868.7 413.4 %all-reduce.18.cloned.1.call-start = ((), (), s32[]{:S(2)}) async-start(), calls=%async_computation.16 | async-start | bytes 1703936 | tf_op jit(solution)/shard_map/psum | solution.py:292
  870.2 1.8 copy-start.20
  878.2 367.9 %copy-start.37 = (bf16[512]{0:T(512)(128)(2,1)S(1)}, bf16[512]{0:T(512)(128)(2,1)}, u32[]{:S(2)}) copy-start(bf16[512]{0:T(512)(128)(2,1)} %get-tuple-element.260) | copy-start | bytes 3076
  878.2 367.9 %copy-start.38 = (bf16[2048]{0:T(1024)(128)(2,1)S(1)}, bf16[2048]{0:T(1024)(128)(2,1)}, u32[]{:S(2)}) copy-start(bf16[2048]{0:T(1024)(128)(2,1)} %get-tuple-element.346) | copy-start | bytes 12292
  878.3 367.8 %copy-start.39 = (bf16[512]{0:T(512)(128)(2,1)S(1)}, bf16[512]{0:T(512)(128)(2,1)}, u32[]{:S(2)}) copy-start(bf16[512]{0:T(512)(128)(2,1)} %get-tuple-element.330) | copy-start | bytes 3076
  878.3 367.8 %copy-start.44 = (bf16[512]{0:T(512)(128)(2,1)S(1)}, bf16[512]{0:T(512)(128)(2,1)}, u32[]{:S(2)}) copy-start(bf16[512]{0:T(512)(128)(2,1)} %get-tuple-element.348) | copy-start | bytes 3076
  878.3 396.7 %copy-start.3 = (f32[1024,512]{0,1:T(8,128)S(1)}, f32[1024,512]{0,1:T(8,128)}, u32[]{:S(2)}) copy-start(f32[1024,512]{0,1:T(8,128)} %copy-done.2) | copy-start | bytes 6291460
  (10 other events, 11.0 us)
Sparse Core Ops, SparseCore 0:
  10.1 58.4 all-gather.3
  70.8 57.5 all-gather.5
  467.5 62.7 reduce-scatter.15
  846.1 62.7 reduce-scatter.7
  912.1 60.9 reduce-scatter.13
  976.7 60.8 reduce-scatter.9
  1041.0 60.9 reduce-scatter.11
  1105.9 66.6 reduce-scatter.19
  1176.5 66.5 reduce-scatter.17
  1246.1 34.6 all-reduce.17
